TPU v7x, 32 devices: a whole 2x2x4 slice. The times are simulated.
32 devices in a mesh: lat: 8 (over y, x, core), lon: 4 (over z).
Axes of the slice: x: 2, y: 2, z: 4, core: 2. Of those that a mesh axis runs over, the one named last changes fastest.
Arguments:
- tracers: float32 [4, 4, 256, 720], P(None, None, 'lat', 'lon'), may hold values from -6 to 6
- courant: float32 [2, 4, 256, 720], P(None, None, 'lat', 'lon'), may hold values from -0.8 to 0.8
- cutoffs: int32 [256], replicated, may hold values from 1 to 360, as said below
Outputs:
- updated: float32 [4, 4, 256, 720], P(None, None, 'lat', 'lon')
- filtered_zonal: float32 [4, 256, 720], P(None, 'lat', 'lon')
Inputs may be any that keep to these rules, and one draw needn't show every extreme that they name: cutoffs[j] is 360 for every row j with min(j, 255 - j) >= 64, below 360 for all other rows, and 1 at the two pole rows.
All inputs are finite; a program needn't handle non-finite values.
Results may differ from a plain program's by a relative error of at most 0.0003.
Values sent between devices are 32-bit elements; how exact they have to be, the bound alone decides.
A program may use at most 64 MiB of HBM per device.

v0:
```python
import math
import jax
import jax.numpy as jnp
from jax import lax
from jax.sharding import PartitionSpec as P


def padded(cells, sides, width, closed):
    for axis, dim in sides:
        count = lax.axis_size(axis)
        ends = count if closed else count - 1
        head = lax.slice_in_dim(cells, 0, width, axis=dim)
        tail = lax.slice_in_dim(cells, cells.shape[dim] - width, cells.shape[dim], axis=dim)
        cells = jnp.concatenate(
            [
                lax.ppermute(tail, axis, [(i, (i + 1) % count) for i in range(ends)]),
                cells,
                lax.ppermute(head, axis, [((i + 1) % count, i) for i in range(ends)]),
            ],
            axis=dim,
        )
    return cells


def take_range(values, start, count, axis_index):
    return lax.slice_in_dim(values, start, start + count, axis=axis_index)


def ppm_flux(extended, courant_faces, axis_index):
    cell_count = extended.shape[axis_index] - 6
    edge_values = 7.0 / 12.0 * (
        take_range(extended, 1, cell_count + 3, axis_index)
        + take_range(extended, 2, cell_count + 3, axis_index)
    ) - 1.0 / 12.0 * (
        take_range(extended, 0, cell_count + 3, axis_index)
        + take_range(extended, 3, cell_count + 3, axis_index)
    )
    left_edge = take_range(edge_values, 0, cell_count + 2, axis_index)
    right_edge = take_range(edge_values, 1, cell_count + 2, axis_index)
    centre = take_range(extended, 2, cell_count + 2, axis_index)
    slopes = right_edge - left_edge
    curvature = 6.0 * centre - 3.0 * (left_edge + right_edge)
    upwind = take_range(right_edge, 0, cell_count + 1, axis_index) - 0.5 * courant_faces * (
        take_range(slopes, 0, cell_count + 1, axis_index)
        - (1.0 - courant_faces * (2.0 / 3.0)) * take_range(curvature, 0, cell_count + 1, axis_index)
    )
    downwind = take_range(left_edge, 1, cell_count + 1, axis_index) - 0.5 * courant_faces * (
        take_range(slopes, 1, cell_count + 1, axis_index)
        + (1.0 + courant_faces * (2.0 / 3.0)) * take_range(curvature, 1, cell_count + 1, axis_index)
    )
    return courant_faces * jnp.where(courant_faces > 0, upwind, downwind)


def metric_weights(first_row, row_count, grid_rows):
    faces = first_row + jnp.arange(-1, row_count, dtype=jnp.int32)
    centres = first_row + jnp.arange(row_count, dtype=jnp.int32)
    face_weight = jnp.sin(
        jnp.minimum(faces + 1, grid_rows - 1 - faces).astype(jnp.float32) * (math.pi / grid_rows)
    )
    cell_weight = jnp.sin(
        (jnp.minimum(centres, grid_rows - 1 - centres).astype(jnp.float32) + 0.5)
        * (math.pi / grid_rows)
    )
    return (face_weight, cell_weight)


def angle_table(first_ids, second_ids, period):
    product = first_ids[:, None] * second_ids[None, :] % period
    angles = product.astype(jnp.float32) * (2.0 * math.pi / period)
    return (jnp.cos(angles), jnp.sin(angles))


def spectral_lowpass(row_block, limits, outer_count):
    row_count, circle = row_block.shape
    inner_count = circle // outer_count
    highest = lax.Precision.HIGHEST
    grid_values = row_block.reshape(row_count, outer_count, inner_count)
    outer_ids = jnp.arange(outer_count, dtype=jnp.int32)
    inner_ids = jnp.arange(inner_count, dtype=jnp.int32)
    outer_cos, outer_sin = angle_table(outer_ids, outer_ids, outer_count)
    inner_cos, inner_sin = angle_table(inner_ids, inner_ids, inner_count)
    twiddle_cos, twiddle_sin = angle_table(inner_ids, outer_ids, circle)
    first_real = jnp.einsum("rab,ak->rbk", grid_values, outer_cos, precision=highest)
    first_imag = -jnp.einsum("rab,ak->rbk", grid_values, outer_sin, precision=highest)
    turned_real = first_real * twiddle_cos + first_imag * twiddle_sin
    turned_imag = first_imag * twiddle_cos - first_real * twiddle_sin
    coeff_real = jnp.einsum("rbk,bj->rjk", turned_real, inner_cos, precision=highest) + jnp.einsum(
        "rbk,bj->rjk", turned_imag, inner_sin, precision=highest
    )
    coeff_imag = jnp.einsum("rbk,bj->rjk", turned_imag, inner_cos, precision=highest) - jnp.einsum(
        "rbk,bj->rjk", turned_real, inner_sin, precision=highest
    )
    wavenumber = inner_ids[:, None] * outer_count + outer_ids[None, :]
    folded = jnp.minimum(wavenumber, circle - wavenumber)
    keep_mask = folded[None, :, :] <= limits[:, None, None]
    coeff_real = jnp.where(keep_mask, coeff_real, 0.0)
    coeff_imag = jnp.where(keep_mask, coeff_imag, 0.0)
    back_real = jnp.einsum("rjk,jb->rbk", coeff_real, inner_cos, precision=highest) - jnp.einsum(
        "rjk,jb->rbk", coeff_imag, inner_sin, precision=highest
    )
    back_imag = jnp.einsum("rjk,jb->rbk", coeff_imag, inner_cos, precision=highest) + jnp.einsum(
        "rjk,jb->rbk", coeff_real, inner_sin, precision=highest
    )
    reverted_real = back_real * twiddle_cos - back_imag * twiddle_sin
    reverted_imag = back_imag * twiddle_cos + back_real * twiddle_sin
    signal = jnp.einsum("rbk,ka->rab", reverted_real, outer_cos, precision=highest) - jnp.einsum(
        "rbk,ka->rab", reverted_imag, outer_sin, precision=highest
    )
    return (signal / circle).reshape(row_count, circle)


def circle_filter(row_block, limits, lon_groups):
    row_count = row_block.shape[0]
    whole_rows = lax.all_to_all(row_block, "lon", split_axis=0, concat_axis=1, tiled=True)
    held_count = row_count // lon_groups
    row_limits = lax.dynamic_slice_in_dim(limits, lax.axis_index("lon") * held_count, held_count)
    lowpass = spectral_lowpass(whole_rows, row_limits, lon_groups)
    lowpass = jnp.where((row_limits < whole_rows.shape[1] // 2)[:, None], lowpass, whole_rows)
    return lax.all_to_all(lowpass, "lon", split_axis=1, concat_axis=0, tiled=True)


def body(tracers, courant, cutoffs):
    levels, tracer_count, lat_rows, lon_cols = tracers.shape
    lon_groups = lax.axis_size("lon")
    lat_bands = lax.axis_size("lat")
    band_index = lax.axis_index("lat")
    grid_rows = lat_rows * lat_bands
    zonal = courant[0]
    meridional = courant[1]
    lat_stack = jnp.concatenate([tracers, meridional[:, None]], axis=1)
    lat_ext = padded(lat_stack, (("lat", 2),), 3, False)
    flat_count = levels * lat_rows
    flat_zonal = zonal.reshape(flat_count, lon_cols)
    local_limits = lax.dynamic_slice_in_dim(cutoffs, band_index * lat_rows, lat_rows)
    filtered_flat = circle_filter(flat_zonal, jnp.tile(local_limits, levels), lon_groups)
    filtered_zonal = filtered_flat.reshape(levels, lat_rows, lon_cols)
    lon_stack = jnp.concatenate([tracers, filtered_zonal[:, None]], axis=1)
    lon_ext = padded(lon_stack, (("lon", 3),), 3, True)
    flux_east = ppm_flux(
        lon_ext[:, :tracer_count], lon_ext[:, tracer_count:, :, 2 : lon_cols + 3], 3
    )
    face_weight, cell_weight = metric_weights(band_index * lat_rows, lat_rows, grid_rows)
    flux_north = (
        ppm_flux(lat_ext[:, :tracer_count], lat_ext[:, tracer_count:, 2 : lat_rows + 3, :], 2)
        * face_weight[None, None, :, None]
    )
    change = (
        flux_east[:, :, :, 1:]
        - flux_east[:, :, :, :-1]
        + (flux_north[:, :, 1:, :] - flux_north[:, :, :-1, :]) / cell_weight[None, None, :, None]
    )
    return (tracers - change, filtered_zonal)


def solution(mesh):
    in_specs = (P(None, None, "lat", "lon"), P(None, None, "lat", "lon"), P())
    out_specs = (P(None, None, "lat", "lon"), P(None, "lat", "lon"))
    return jax.shard_map(body, mesh=mesh, in_specs=in_specs, out_specs=out_specs, check_vma=False)
```

profile of v0, /device:TPU:0, one launch (start us, length us, event | category | flops | bytes accessed | tf_op | source)
XLA Modules:
  0.0 59.9 jit_solution(16525917794037167420)
XLA Ops:
  0.6 1.7 %slice_bitcast_fusion.1 = (f32[4,32,180]{2,1,0:T(8,128)}, f32[4,1,32,180]{3,2,1,0:T(8,128)S(1)}) fusion(f32[2,4,32,180]{3,2,1,0:T(8,128)} %param.4), kind=kLoop, calls=%fused_computation.113 | loop fusion | bytes 368640 | tf_op jit(solution)/shard_map/all_to_all | solution.py:114
  2.4 1.3 %collective-permute-start.3 = (f32[4,5,3,180]{3,2,1,0:T(4,128)S(1)}, f32[4,5,3,180]{3,2,1,0:T(4,128)S(1)}, u32[]{:S(2)}, u32[]{:S(2)}) collective-permute-start(f32[4,5,3,180]{3,2,1,0:T(4,128)S(1)} %get-tuple-element.15), channel_id=1, source_target_pairs={{4,0},{8,4},{12,8},{16,12},{20,16},{24,20},{28,24},{5,1},{9,5},{13... | collective-permute-start | bytes 129608 | tf_op jit(solution)/shard_map/ppermute | solution.py:18
  3.7 3.0 %collective-permute-start.2 = (f32[4,5,3,180]{3,2,1,0:T(4,128)S(1)}, f32[4,5,3,180]{3,2,1,0:T(4,128)S(1)}, u32[]{:S(2)}, u32[]{:S(2)}) collective-permute-start(f32[4,5,3,180]{3,2,1,0:T(4,128)S(1)} %get-tuple-element.14), channel_id=1, source_target_pairs={{0,4},{4,8},{8,12},{12,16},{16,20},{20,24},{24,28},{1,5},{5,9},{9,... | collective-permute-start | bytes 129608 | tf_op jit(solution)/shard_map/ppermute | solution.py:16
  6.7 6.4 %all-to-all-start = ((f32[4,32,180]{2,1,0:T(8,128)}), f32[4,32,180]{2,1,0:T(8,128)S(1)}, u32[]{:S(2)}, u32[]{:S(2)}) async-start(f32[4,32,180]{2,1,0:T(8,128)} %get-tuple-element.22), calls=%async_computation | async-start | bytes 262144 | tf_op jit(solution)/shard_map/all_to_all | solution.py:114
  13.2 0.7 %copy-done.1 = s32[256]{0:T(256)S(1)} copy-done((s32[256]{0:T(256)S(1)}, s32[256]{0:T(256)}, u32[]{:S(2)}) %copy-start.1) | copy-done | bytes 1048
  14.9 4.8 %all-to-all-done = f32[4,32,180]{2,1,0:T(8,128)S(1)} async-done(((f32[4,32,180]{2,1,0:T(8,128)}), f32[4,32,180]{2,1,0:T(8,128)S(1)}, u32[]{:S(2)}, u32[]{:S(2)}) %all-to-all-start) | async-done | bytes 92192 | tf_op jit(solution)/shard_map/all_to_all | solution.py:114
  19.7 0.4 convolution_bitcast_fusion
  20.1 0.4 multiply_add_fusion
  20.6 1.0 %fusion.47 = f32[180,32,4]{0,1,2:T(8,128)S(1)} fusion(f32[32,180,4]{1,2,0:T(4,128)S(1)} %get-tuple-element.21), kind=kOutput, calls=%fused_computation.82 | convolution fusion | flops 50058000 | bytes 184320 | tf_op jit(solution)/shard_map/rbk,bj->rjk/dot_general | solution.py:90
  21.6 1.0 %fusion.51 = f32[180,32,4]{0,1,2:T(8,128)S(1)} fusion(f32[32,180,4]{1,2,0:T(4,128)S(1)} %get-tuple-element.20), kind=kOutput, calls=%fused_computation.86 | convolution fusion | flops 50058000 | bytes 184320 | tf_op jit(solution)/shard_map/rbk,bj->rjk/dot_general | solution.py:87
  22.7 1.1 %fusion.5 = f32[32,180,4]{1,0,2:T(8,128)S(1)} fusion(f32[180,32,4]{0,1,2:T(8,128)S(1)} %fusion.47, f32[32,180,4]{1,2,0:T(4,128)S(1)} %get-tuple-element.20, s32[180,4]{0,1:T(4,128)S(1)} %subtract_minimum_fusion, s32[32]{0:T(128)S(1)} %get-tuple-element.7), kind=kOutput, calls=%fused_computation.11 | convolution fusion | flops 50127120 | bytes 279488 | tf_op jit(solution)/shard_map/rbk,bj->rjk/dot_general | solution.py:90
  23.8 1.1 %fusion.45 = f32[180,32,4]{0,1,2:T(8,128)S(1)} fusion(f32[32,180,4]{1,0,2:T(8,128)S(1)} %fusion.5), kind=kOutput, calls=%fused_computation.80 | convolution fusion | flops 50058000 | bytes 184320 | tf_op jit(solution)/shard_map/rjk,jb->rbk/dot_general | solution.py:101
  24.8 1.0 %fusion.7 = f32[32,180,4]{1,0,2:T(8,128)S(1)} fusion(f32[180,32,4]{0,1,2:T(8,128)S(1)} %fusion.51, f32[32,180,4]{1,2,0:T(4,128)S(1)} %get-tuple-element.21, s32[180,4]{0,1:T(4,128)S(1)} %subtract_minimum_fusion, s32[32]{0:T(128)S(1)} %get-tuple-element.7), kind=kOutput, calls=%fused_computation.14 | convolution fusion | flops 50127120 | bytes 279488 | tf_op jit(solution)/shard_map/rbk,bj->rjk/dot_general | solution.py:87
  25.9 1.0 %fusion.49 = f32[180,32,4]{0,1,2:T(8,128)S(1)} fusion(f32[32,180,4]{1,0,2:T(8,128)S(1)} %fusion.7), kind=kOutput, calls=%fused_computation.84 | convolution fusion | flops 50058000 | bytes 184320 | tf_op jit(solution)/shard_map/rjk,jb->rbk/dot_general | solution.py:98
  26.9 1.1 %convolution_add_fusion = f32[180,32,4]{0,1,2:T(8,128)S(1)} fusion(f32[180,32,4]{0,1,2:T(8,128)S(1)} %fusion.45, f32[32,180,4]{1,0,2:T(8,128)S(1)} %fusion.7), kind=kOutput, calls=%fused_computation.7 | convolution fusion | flops 50081040 | bytes 276480 | tf_op jit(solution)/shard_map/rjk,jb->rbk/dot_general | solution.py:101
  28.0 1.1 %add_bitcast_fusion.2 = (f32[32,180,4]{1,0,2:T(8,128)S(1)}, f32[32,180,4]{1,0,2:T(8,128)S(1)}) fusion(f32[180,32,4]{0,1,2:T(8,128)S(1)} %convolution_add_fusion, f32[180,4]{0,1:T(4,128)S(1)} %get-tuple-element.30, f32[180,4]{0,1:T(4,128)S(1)} %get-tuple-element.31, f32[180,32,4]{0,1,2:T(8,128)S(1)} %fusion.49, f32[32,180,4]{1,0,2:T(8,128)S(1)} %fusion.5), kind=kOutput, calls=%fused_computation.109 | convolution fusion | flops 50219280 | bytes 466560 | tf_op jit(solution)/shard_map/rjk,jb->rbk/dot_general | solution.py:98
  29.0 0.4 fusion.69
  29.5 0.5 fusion.3
  30.0 0.7 %copy.21 = f32[32,4,180]{2,0,1:T(8,128)} copy(f32[32,4,180]{2,1,0:T(4,128)S(1)} %fusion.3) | data formatting | bytes 184320 | tf_op jit(solution)/shard_map/jit(_where)/select_n | solution.py:118
  30.6 3.4 %all-to-all-start.1 = ((f32[32,4,180]{2,0,1:T(8,128)}), f32[32,4,180]{2,0,1:T(8,128)S(1)}, u32[]{:S(2)}, u32[]{:S(2)}) async-start(f32[32,4,180]{2,0,1:T(8,128)} %copy.21), calls=%async_computation.1 | async-start | bytes 262144 | tf_op jit(solution)/shard_map/all_to_all | solution.py:119
  34.1 6.2 %all-to-all-done.1 = f32[32,4,180]{2,0,1:T(8,128)S(1)} async-done(((f32[32,4,180]{2,0,1:T(8,128)}), f32[32,4,180]{2,0,1:T(8,128)S(1)}, u32[]{:S(2)}, u32[]{:S(2)}) %all-to-all-start.1) | async-done | bytes 92192 | tf_op jit(solution)/shard_map/all_to_all | solution.py:119
  40.4 1.7 %collective-permute-start.1 = (f32[4,5,32,3]{3,2,1,0:T(8,128)S(1)}, f32[4,5,32,3]{3,2,1,0:T(8,128)S(1)}, u32[]{:S(2)}, u32[]{:S(2)}) collective-permute-start(f32[4,5,32,3]{3,2,1,0:T(8,128)S(1)} %get-tuple-element.11), channel_id=1, source_target_pairs={{1,0},{2,1},{3,2},{0,3},{5,4},{6,5},{7,6},{4,7},{9,8},{10,9},{11,1... | collective-permute-start | bytes 23048 | tf_op jit(solution)/shard_map/ppermute | solution.py:18
  42.1 0.4 collective-permute-start
  42.5 0.4 fusion.13
  42.9 7.3 %collective-permute-done.1 = f32[4,5,32,3]{3,2,1,0:T(8,128)S(1)} collective-permute-done((f32[4,5,32,3]{3,2,1,0:T(8,128)S(1)}, f32[4,5,32,3]{3,2,1,0:T(8,128)S(1)}, u32[]{:S(2)}, u32[]{:S(2)}) %collective-permute-start.1) | collective-permute-done | bytes 7712 | tf_op jit(solution)/shard_map/ppermute | solution.py:18
  50.2 6.2 %collective-permute-done = f32[4,5,32,3]{3,2,1,0:T(8,128)S(1)} collective-permute-done((f32[4,5,32,3]{3,2,1,0:T(8,128)S(1)}, f32[4,5,32,3]{3,2,1,0:T(8,128)S(1)}, u32[]{:S(2)}, u32[]{:S(2)}) %collective-permute-start) | collective-permute-done | bytes 7712 | tf_op jit(solution)/shard_map/ppermute | solution.py:16
  56.4 0.3 pad_maximum_fusion.5
  56.7 0.5 fusion.36
  57.3 0.3 slice_subtract_fusion.3
  57.8 0.5 fusion.29
  58.3 1.0 %fusion.24 = f32[4,4,32,180]{3,2,1,0:T(8,128)} fusion(f32[4,4,32,180]{3,2,1,0:T(8,128)S(1)} %copy-done, f32[4,4,33,180]{3,2,1,0:T(8,128)S(1)} %fusion.13, f32[4,4,32,181]{3,2,1,0:T(8,128)S(1)} %fusion.29, f32[32]{0:T(128)S(1)} %fusion.125), kind=kLoop, calls=%fused_computation.47 | loop fusion | flops 460800 | bytes 2211968 | tf_op jit(solution)/shard_map/sub | solution.py:152
  59.3 0.7 %copy.47 = f32[4,32,180]{2,1,0:T(8,128)} copy(f32[4,32,180]{2,1,0:T(8,128)S(1)} %bitcast.95) | data formatting | bytes 184320
  (23 shorter events, 1.4 us)
Async XLA Ops:
  0.6 1.7 %copy-start = (f32[4,4,32,180]{3,2,1,0:T(8,128)S(1)}, f32[4,4,32,180]{3,2,1,0:T(8,128)}, u32[]{:S(2)}) copy-start(f32[4,4,32,180]{3,2,1,0:T(8,128)} %param.3) | copy-start | bytes 1105924
  2.4 11.8 %collective-permute-start.3 = (f32[4,5,3,180]{3,2,1,0:T(4,128)S(1)}, f32[4,5,3,180]{3,2,1,0:T(4,128)S(1)}, u32[]{:S(2)}, u32[]{:S(2)}) collective-permute-start(f32[4,5,3,180]{3,2,1,0:T(4,128)S(1)} %get-tuple-element.15), channel_id=1, source_target_pairs={{4,0},{8,4},{12,8},{16,12},{20,16},{24,20},{28,24},{5,1},{9,5},{13... | collective-permute-start | bytes 129608 | tf_op jit(solution)/shard_map/ppermute | solution.py:18
  3.7 10.5 %collective-permute-start.2 = (f32[4,5,3,180]{3,2,1,0:T(4,128)S(1)}, f32[4,5,3,180]{3,2,1,0:T(4,128)S(1)}, u32[]{:S(2)}, u32[]{:S(2)}) collective-permute-start(f32[4,5,3,180]{3,2,1,0:T(4,128)S(1)} %get-tuple-element.14), channel_id=1, source_target_pairs={{0,4},{4,8},{8,12},{12,16},{16,20},{20,24},{24,28},{1,5},{5,9},{9,... | collective-permute-start | bytes 129608 | tf_op jit(solution)/shard_map/ppermute | solution.py:16
  6.7 13.0 %all-to-all-start = ((f32[4,32,180]{2,1,0:T(8,128)}), f32[4,32,180]{2,1,0:T(8,128)S(1)}, u32[]{:S(2)}, u32[]{:S(2)}) async-start(f32[4,32,180]{2,1,0:T(8,128)} %get-tuple-element.22), calls=%async_computation | async-start | bytes 262144 | tf_op jit(solution)/shard_map/all_to_all | solution.py:114
  13.2 0.7 %copy-start.1 = (s32[256]{0:T(256)S(1)}, s32[256]{0:T(256)}, u32[]{:S(2)}) copy-start(s32[256]{0:T(256)} %param.5) | copy-start | bytes 3076
  30.6 9.6 %all-to-all-start.1 = ((f32[32,4,180]{2,0,1:T(8,128)}), f32[32,4,180]{2,0,1:T(8,128)S(1)}, u32[]{:S(2)}, u32[]{:S(2)}) async-start(f32[32,4,180]{2,0,1:T(8,128)} %copy.21), calls=%async_computation.1 | async-start | bytes 262144 | tf_op jit(solution)/shard_map/all_to_all | solution.py:119
  40.4 9.8 %collective-permute-start.1 = (f32[4,5,32,3]{3,2,1,0:T(8,128)S(1)}, f32[4,5,32,3]{3,2,1,0:T(8,128)S(1)}, u32[]{:S(2)}, u32[]{:S(2)}) collective-permute-start(f32[4,5,32,3]{3,2,1,0:T(8,128)S(1)} %get-tuple-element.11), channel_id=1, source_target_pairs={{1,0},{2,1},{3,2},{0,3},{5,4},{6,5},{7,6},{4,7},{9,8},{10,9},{11,1... | collective-permute-start | bytes 23048 | tf_op jit(solution)/shard_map/ppermute | solution.py:18
  42.1 14.3 %collective-permute-start = (f32[4,5,32,3]{3,2,1,0:T(8,128)S(1)}, f32[4,5,32,3]{3,2,1,0:T(8,128)S(1)}, u32[]{:S(2)}, u32[]{:S(2)}) collective-permute-start(f32[4,5,32,3]{3,2,1,0:T(8,128)S(1)} %get-tuple-element.10), channel_id=1, source_target_pairs={{0,1},{1,2},{2,3},{3,0},{4,5},{5,6},{6,7},{7,4},{8,9},{9,10},{10,1... | collective-permute-start | bytes 23048 | tf_op jit(solution)/shard_map/ppermute | solution.py:16
where the time goes:
time: 60.3 us; the launch traced here: 59.9 us
  waiting for transfers between devices  24.5 us (41%)
  starting transfers between devices  16.2 us (27%)
  matrix products  10.1 us (17%)
  other arithmetic  4.35 us (7%)
  local copies, waits for them, and re-layouts  3.88 us (6%)
  between operations  0.88 us (1%)
    ppermute x2, waiting for transfers between devices, padded(): lax.ppermute(head, axis, [((i + 1) % count, i) for i in range(ends)])  7.29 us
    all_to_all x1, starting transfers between devices, circle_filter(): lax.all_to_all(row_block, 'lon', split_axis=0, concat_axis=1, tiled=True)  6.36 us
    ppermute x2, waiting for transfers between devices, padded(): lax.ppermute(tail, axis, [(i, (i + 1) % count) for i in range(ends)])  6.19 us
    all_to_all x1, waiting for transfers between devices, circle_filter(): lax.all_to_all(lowpass, 'lon', split_axis=1, concat_axis=0, tiled=True)  6.16 us
    all_to_all x1, waiting for transfers between devices, circle_filter(): lax.all_to_all(row_block, 'lon', split_axis=0, concat_axis=1, tiled=True)  4.84 us
    ppermute x2, starting transfers between devices, padded(): lax.ppermute(tail, axis, [(i, (i + 1) % count) for i in range(ends)])  3.45 us
    all_to_all x1, starting transfers between devices, circle_filter(): lax.all_to_all(lowpass, 'lon', split_axis=1, concat_axis=0, tiled=True)  3.43 us
    ppermute x2, starting transfers between devices, padded(): lax.ppermute(head, axis, [((i + 1) % count, i) for i in range(ends)])  2.95 us
  transfers between devices with their start and end apart: 6, of which 4 were waited for; matrix products, arithmetic and copies ran while one was open for 2% of the time, Pallas kernels for 0%

commit v1 on v0

--- a/solution.py
+++ b/solution.py
@@ -3,6 +3,17 @@
 import jax.numpy as jnp
 from jax import lax
 from jax.sharding import PartitionSpec as P
+
+
+def in_blocks(value, dim, peers):
+    before, after = (value.shape[:dim], value.shape[dim + 1 :])
+    return jnp.moveaxis(value.reshape(*before, peers, -1, *after), dim, 0)
+
+
+def joined_along(parts, dim):
+    parts = jnp.moveaxis(parts, 0, dim)
+    dims = parts.shape
+    return parts.reshape(*dims[:dim], dims[dim] * dims[dim + 1], *dims[dim + 2 :])
 
 
 def padded(cells, sides, width, closed):
@@ -111,7 +122,14 @@
 
 def circle_filter(row_block, limits, lon_groups):
     row_count = row_block.shape[0]
-    whole_rows = lax.all_to_all(row_block, "lon", split_axis=0, concat_axis=1, tiled=True)
+    count_2, position = (lax.axis_size("lon"), lax.axis_index("lon"))
+    pieces = in_blocks(row_block, 0, count_2)
+    outs = [pieces[position]]
+    for step in range(1, count_2):
+        sent = pieces[position ^ step]
+        outs.append(lax.ppermute(sent, "lon", [(i_2, i_2 ^ step) for i_2 in range(count_2)]))
+    pieces = jnp.stack(outs)[position ^ jnp.arange(count_2)]
+    whole_rows = joined_along(pieces, 1)
     held_count = row_count // lon_groups
     row_limits = lax.dynamic_slice_in_dim(limits, lax.axis_index("lon") * held_count, held_count)
     lowpass = spectral_lowpass(whole_rows, row_limits, lon_groups)

time: 60.3 us -> 57.6 us (0.955)
  waiting for transfers between devices: 24.5 us -> 22.4 us
  starting transfers between devices: 16.2 us -> 15.5 us
    all_to_all x1 -> x0, starting transfers between devices: 6.36 us -> none  [circle_filter(): lax.all_to_all(row_block, 'lon', split_axis=0, concat_axis=1, tiled=True)]
    ppermute x0 -> x3, starting transfers between devices: none -> 5.78 us  [circle_filter(): lax.ppermute(sent, 'lon', [(i_2, i_2 ^ step) for i_2 in range(count_2)])]
    all_to_all x1 -> x0, waiting for transfers between devices: 4.84 us -> none  [circle_filter(): lax.all_to_all(row_block, 'lon', split_axis=0, concat_axis=1, tiled=True)]
    ppermute x0 -> x3, waiting for transfers between devices: none -> 3.24 us  [circle_filter(): lax.ppermute(sent, 'lon', [(i_2, i_2 ^ step) for i_2 in range(count_2)])]
    all_to_all x1 -> x0, local copies, waits for them, and re-layouts: 1.7 us -> none  [circle_filter(): lax.all_to_all(row_block, 'lon', split_axis=0, concat_axis=1, tiled=True)]
    slice x0 -> x1, local copies, waits for them, and re-layouts: none -> 1.04 us  [body(): zonal = courant[0]]
  transfers between devices with their start and end apart: 6 -> 8, of which waited for: 4 -> 5; matrix products, arithmetic and copies ran while one was open for 2% -> 23% of each run, Pallas kernels for 0% -> 0%
where the time goes in v1:
time: 57.6 us; the launch traced here: 57.3 us
  waiting for transfers between devices  22.4 us (39%)
  starting transfers between devices  15.5 us (27%)
  matrix products  10.2 us (18%)
  other arithmetic  4.38 us (8%)
  local copies, waits for them, and re-layouts  3.9 us (7%)
  between operations  0.95 us (2%)
    ppermute x2, waiting for transfers between devices, padded(): lax.ppermute(head, axis, [((i + 1) % count, i) for i in range(ends)])  7.29 us
    ppermute x2, waiting for transfers between devices, padded(): lax.ppermute(tail, axis, [(i, (i + 1) % count) for i in range(ends)])  6.26 us
    ppermute x3, starting transfers between devices, circle_filter(): lax.ppermute(sent, 'lon', [(i_2, i_2 ^ step) for i_2 in range(count_2)])  5.78 us
    all_to_all x1, waiting for transfers between devices, circle_filter(): lax.all_to_all(lowpass, 'lon', split_axis=1, concat_axis=0, tiled=True)  5.58 us
    ppermute x2, starting transfers between devices, padded(): lax.ppermute(tail, axis, [(i, (i + 1) % count) for i in range(ends)])  3.45 us
    all_to_all x1, starting transfers between devices, circle_filter(): lax.all_to_all(lowpass, 'lon', split_axis=1, concat_axis=0, tiled=True)  3.33 us
    ppermute x3, waiting for transfers between devices, circle_filter(): lax.ppermute(sent, 'lon', [(i_2, i_2 ^ step) for i_2 in range(count_2)])  3.24 us
    ppermute x2, starting transfers between devices, padded(): lax.ppermute(head, axis, [((i + 1) % count, i) for i in range(ends)])  2.95 us
  transfers between devices with their start and end apart: 8, of which 5 were waited for; matrix products, arithmetic and copies ran while one was open for 23% of the time, Pallas kernels for 0%

profile of v1, /device:TPU:0, one launch (start us, length us, event | category | flops | bytes accessed | tf_op | source)
XLA Modules:
  0.0 57.3 jit_solution(9671600675421786162)
XLA Ops:
  0.6 1.0 %fusion.164 = (f32[1,4,32,180]{3,2,1,0:T(8,128)S(1)}, f32[4,1,32,180]{3,2,1,0:T(8,128)S(1)}) fusion(f32[2,4,32,180]{3,2,1,0:T(8,128)} %param.4), kind=kLoop, calls=%fused_computation.213 | loop fusion | bytes 368640 | tf_op jit(solution)/shard_map/slice | solution.py:146
  1.8 1.3 %collective-permute-start.6 = (f32[4,5,3,180]{3,2,1,0:T(4,128)S(1)}, f32[4,5,3,180]{3,2,1,0:T(4,128)S(1)}, u32[]{:S(2)}, u32[]{:S(2)}) collective-permute-start(f32[4,5,3,180]{3,2,1,0:T(4,128)S(1)} %get-tuple-element.17), channel_id=1, source_target_pairs={{4,0},{8,4},{12,8},{16,12},{20,16},{24,20},{28,24},{5,1},{9,5},{13... | collective-permute-start | bytes 129608 | tf_op jit(solution)/shard_map/ppermute | solution.py:29
  3.1 3.0 %collective-permute-start.5 = (f32[4,5,3,180]{3,2,1,0:T(4,128)S(1)}, f32[4,5,3,180]{3,2,1,0:T(4,128)S(1)}, u32[]{:S(2)}, u32[]{:S(2)}) collective-permute-start(f32[4,5,3,180]{3,2,1,0:T(4,128)S(1)} %get-tuple-element.16), channel_id=1, source_target_pairs={{0,4},{4,8},{8,12},{12,16},{16,20},{20,24},{24,28},{1,5},{5,9},{9,... | collective-permute-start | bytes 129608 | tf_op jit(solution)/shard_map/ppermute | solution.py:27
  6.2 5.1 %collective-permute-start.2 = (f32[32,180]{1,0:T(8,128)S(1)}, f32[32,180]{1,0:T(8,128)S(1)}, u32[]{:S(2)}, u32[]{:S(2)}) collective-permute-start(f32[32,180]{1,0:T(8,128)S(1)} %get-tuple-element.31), channel_id=1, source_target_pairs={{0,3},{1,2},{2,1},{3,0},{4,7},{5,6},{6,5},{7,4},{8,11},{9,10},{10,... | collective-permute-start | bytes 69128 | tf_op jit(solution)/shard_map/ppermute | solution.py:130
  11.4 0.6 %collective-permute-start = (f32[32,180]{1,0:T(8,128)S(1)}, f32[32,180]{1,0:T(8,128)S(1)}, u32[]{:S(2)}, u32[]{:S(2)}) collective-permute-start(f32[32,180]{1,0:T(8,128)S(1)} %get-tuple-element.33), channel_id=1, source_target_pairs={{0,1},{1,0},{2,3},{3,2},{4,5},{5,4},{6,7},{7,6},{8,9},{9,8},{10,11... | collective-permute-start | bytes 69128 | tf_op jit(solution)/shard_map/ppermute | solution.py:130
  12.2 0.7 %copy-done.1 = s32[256]{0:T(256)S(1)} copy-done((s32[256]{0:T(256)S(1)}, s32[256]{0:T(256)}, u32[]{:S(2)}) %copy-start.1) | copy-done | bytes 1048
  13.4 3.0 %collective-permute-done.1 = f32[32,180]{1,0:T(8,128)S(1)} collective-permute-done((f32[32,180]{1,0:T(8,128)S(1)}, f32[32,180]{1,0:T(8,128)S(1)}, u32[]{:S(2)}, u32[]{:S(2)}) %collective-permute-start.1) | collective-permute-done | bytes 23072 | tf_op jit(solution)/shard_map/ppermute | solution.py:130
  16.4 0.6 gather_fusion
  17.0 0.4 fusion.67
  17.4 0.4 fusion.65
  17.9 1.1 %fusion.46 = f32[180,32,4]{0,1,2:T(8,128)S(1)} fusion(f32[32,180,4]{1,2,0:T(4,128)S(1)} %fusion.67, f32[32,180,4]{1,2,0:T(4,128)S(1)} %fusion.65, f32[180,4]{0,1:T(4,128)S(1)} %get-tuple-element.34, f32[180,4]{0,1:T(4,128)S(1)} %get-tuple-element.35), kind=kOutput, calls=%fused_computation.80 | convolution fusion | flops 50150160 | bytes 282240 | tf_op jit(solution)/shard_map/rbk,bj->rjk/dot_general | solution.py:101
  18.9 1.0 %fusion.50 = f32[180,32,4]{0,1,2:T(8,128)S(1)} fusion(f32[32,180,4]{1,2,0:T(4,128)S(1)} %fusion.67, f32[32,180,4]{1,2,0:T(4,128)S(1)} %fusion.65, f32[180,4]{0,1:T(4,128)S(1)} %get-tuple-element.34, f32[180,4]{0,1:T(4,128)S(1)} %get-tuple-element.35), kind=kOutput, calls=%fused_computation.84 | convolution fusion | flops 50150160 | bytes 282240 | tf_op jit(solution)/shard_map/rbk,bj->rjk/dot_general | solution.py:98
  20.0 1.1 %fusion.4 = f32[32,180,4]{1,0,2:T(8,128)S(1)} fusion(f32[180,32,4]{0,1,2:T(8,128)S(1)} %fusion.46, s32[180,4]{0,1:T(4,128)S(1)} %subtract_minimum_fusion, s32[32]{0:T(128)S(1)} %get-tuple-element.9, f32[32,180,4]{1,2,0:T(4,128)S(1)} %fusion.67, f32[32,180,4]{1,2,0:T(4,128)S(1)} %fusion.65, f32[180,4]{0,1:T(4,128)S(1)} %get-tuple-element.34, ...), kind=kOutput, calls=%fused_computation.9 | convolution fusion | flops 50219280 | bytes 377408 | tf_op jit(solution)/shard_map/rbk,bj->rjk/dot_general | solution.py:101
  21.0 1.0 %fusion.44 = f32[180,32,4]{0,1,2:T(8,128)S(1)} fusion(f32[32,180,4]{1,0,2:T(8,128)S(1)} %fusion.4), kind=kOutput, calls=%fused_computation.78 | convolution fusion | flops 50058000 | bytes 184320 | tf_op jit(solution)/shard_map/rjk,jb->rbk/dot_general | solution.py:112
  22.1 1.1 %fusion.6 = f32[32,180,4]{1,0,2:T(8,128)S(1)} fusion(f32[180,32,4]{0,1,2:T(8,128)S(1)} %fusion.50, s32[180,4]{0,1:T(4,128)S(1)} %subtract_minimum_fusion, s32[32]{0:T(128)S(1)} %get-tuple-element.9, f32[32,180,4]{1,2,0:T(4,128)S(1)} %fusion.67, f32[32,180,4]{1,2,0:T(4,128)S(1)} %fusion.65, f32[180,4]{0,1:T(4,128)S(1)} %get-tuple-element.34, ...), kind=kOutput, calls=%fused_computation.12 | convolution fusion | flops 50219280 | bytes 377408 | tf_op jit(solution)/shard_map/rbk,bj->rjk/dot_general | solution.py:98
  23.2 1.0 %fusion.48 = f32[180,32,4]{0,1,2:T(8,128)S(1)} fusion(f32[32,180,4]{1,0,2:T(8,128)S(1)} %fusion.6), kind=kOutput, calls=%fused_computation.82 | convolution fusion | flops 50058000 | bytes 184320 | tf_op jit(solution)/shard_map/rjk,jb->rbk/dot_general | solution.py:109
  24.2 1.0 %convolution_add_fusion = f32[180,32,4]{0,1,2:T(8,128)S(1)} fusion(f32[180,32,4]{0,1,2:T(8,128)S(1)} %fusion.44, f32[32,180,4]{1,0,2:T(8,128)S(1)} %fusion.6), kind=kOutput, calls=%fused_computation.5 | convolution fusion | flops 50081040 | bytes 276480 | tf_op jit(solution)/shard_map/rjk,jb->rbk/dot_general | solution.py:112
  25.3 1.1 %add_bitcast_fusion.2 = (f32[32,180,4]{1,0,2:T(8,128)S(1)}, f32[32,180,4]{1,0,2:T(8,128)S(1)}) fusion(f32[180,32,4]{0,1,2:T(8,128)S(1)} %convolution_add_fusion, f32[180,4]{0,1:T(4,128)S(1)} %get-tuple-element.34, f32[180,4]{0,1:T(4,128)S(1)} %get-tuple-element.35, f32[180,32,4]{0,1,2:T(8,128)S(1)} %fusion.48, f32[32,180,4]{1,0,2:T(8,128)S(1)} %fusion.4), kind=kOutput, calls=%fused_computation.111 | convolution fusion | flops 50219280 | bytes 466560 | tf_op jit(solution)/shard_map/rjk,jb->rbk/dot_general | solution.py:109
  26.3 0.4 fusion.70
  26.8 0.5 fusion.2
  27.2 0.7 %copy.37 = f32[32,4,180]{2,0,1:T(8,128)} copy(f32[32,4,180]{2,1,0:T(4,128)S(1)} %fusion.2) | data formatting | bytes 184320 | tf_op jit(solution)/shard_map/jit(_where)/select_n | solution.py:136
  27.9 3.3 %all-to-all-start = ((f32[32,4,180]{2,0,1:T(8,128)}), f32[32,4,180]{2,0,1:T(8,128)S(1)}, u32[]{:S(2)}, u32[]{:S(2)}) async-start(f32[32,4,180]{2,0,1:T(8,128)} %copy.37), calls=%async_computation | async-start | bytes 262144 | tf_op jit(solution)/shard_map/all_to_all | solution.py:137
  32.0 5.6 %all-to-all-done = f32[32,4,180]{2,0,1:T(8,128)S(1)} async-done(((f32[32,4,180]{2,0,1:T(8,128)}), f32[32,4,180]{2,0,1:T(8,128)S(1)}, u32[]{:S(2)}, u32[]{:S(2)}) %all-to-all-start) | async-done | bytes 92192 | tf_op jit(solution)/shard_map/all_to_all | solution.py:137
  37.7 1.7 %collective-permute-start.4 = (f32[4,5,32,3]{3,2,1,0:T(8,128)S(1)}, f32[4,5,32,3]{3,2,1,0:T(8,128)S(1)}, u32[]{:S(2)}, u32[]{:S(2)}) collective-permute-start(f32[4,5,32,3]{3,2,1,0:T(8,128)S(1)} %get-tuple-element.13), channel_id=1, source_target_pairs={{1,0},{2,1},{3,2},{0,3},{5,4},{6,5},{7,6},{4,7},{9,8},{10,9},{11,1... | collective-permute-start | bytes 23048 | tf_op jit(solution)/shard_map/ppermute | solution.py:29
  39.4 0.4 collective-permute-start.3
  39.8 0.4 fusion.12
  40.2 7.3 %collective-permute-done.4 = f32[4,5,32,3]{3,2,1,0:T(8,128)S(1)} collective-permute-done((f32[4,5,32,3]{3,2,1,0:T(8,128)S(1)}, f32[4,5,32,3]{3,2,1,0:T(8,128)S(1)}, u32[]{:S(2)}, u32[]{:S(2)}) %collective-permute-start.4) | collective-permute-done | bytes 7712 | tf_op jit(solution)/shard_map/ppermute | solution.py:29
  47.5 6.3 %collective-permute-done.3 = f32[4,5,32,3]{3,2,1,0:T(8,128)S(1)} collective-permute-done((f32[4,5,32,3]{3,2,1,0:T(8,128)S(1)}, f32[4,5,32,3]{3,2,1,0:T(8,128)S(1)}, u32[]{:S(2)}, u32[]{:S(2)}) %collective-permute-start.3) | collective-permute-done | bytes 7712 | tf_op jit(solution)/shard_map/ppermute | solution.py:27
  54.1 0.5 fusion.35
  55.1 0.5 fusion.28
  55.6 1.0 %fusion.23 = f32[4,4,32,180]{3,2,1,0:T(8,128)} fusion(f32[4,4,32,180]{3,2,1,0:T(8,128)S(1)} %copy-done, f32[4,4,33,180]{3,2,1,0:T(8,128)S(1)} %fusion.12, f32[4,4,32,181]{3,2,1,0:T(8,128)S(1)} %fusion.28, f32[32]{0:T(128)S(1)} %fusion.134), kind=kLoop, calls=%fused_computation.45 | loop fusion | flops 460800 | bytes 2211968 | tf_op jit(solution)/shard_map/sub | solution.py:170
  56.6 0.7 %copy.68 = f32[4,32,180]{2,1,0:T(8,128)} copy(f32[4,32,180]{2,1,0:T(8,128)S(1)} %bitcast.98) | data formatting | bytes 184320
  (32 shorter events, 2.4 us)
Async XLA Ops:
  0.6 1.2 %copy-start = (f32[4,4,32,180]{3,2,1,0:T(8,128)S(1)}, f32[4,4,32,180]{3,2,1,0:T(8,128)}, u32[]{:S(2)}) copy-start(f32[4,4,32,180]{3,2,1,0:T(8,128)} %param.3) | copy-start | bytes 1105924
  1.8 29.4 %collective-permute-start.6 = (f32[4,5,3,180]{3,2,1,0:T(4,128)S(1)}, f32[4,5,3,180]{3,2,1,0:T(4,128)S(1)}, u32[]{:S(2)}, u32[]{:S(2)}) collective-permute-start(f32[4,5,3,180]{3,2,1,0:T(4,128)S(1)} %get-tuple-element.17), channel_id=1, source_target_pairs={{4,0},{8,4},{12,8},{16,12},{20,16},{24,20},{28,24},{5,1},{9,5},{13... | collective-permute-start | bytes 129608 | tf_op jit(solution)/shard_map/ppermute | solution.py:29
  3.1 28.1 %collective-permute-start.5 = (f32[4,5,3,180]{3,2,1,0:T(4,128)S(1)}, f32[4,5,3,180]{3,2,1,0:T(4,128)S(1)}, u32[]{:S(2)}, u32[]{:S(2)}) collective-permute-start(f32[4,5,3,180]{3,2,1,0:T(4,128)S(1)} %get-tuple-element.16), channel_id=1, source_target_pairs={{0,4},{4,8},{8,12},{12,16},{16,20},{20,24},{24,28},{1,5},{5,9},{9,... | collective-permute-start | bytes 129608 | tf_op jit(solution)/shard_map/ppermute | solution.py:27
  6.2 7.1 %collective-permute-start.2 = (f32[32,180]{1,0:T(8,128)S(1)}, f32[32,180]{1,0:T(8,128)S(1)}, u32[]{:S(2)}, u32[]{:S(2)}) collective-permute-start(f32[32,180]{1,0:T(8,128)S(1)} %get-tuple-element.31), channel_id=1, source_target_pairs={{0,3},{1,2},{2,1},{3,0},{4,7},{5,6},{6,5},{7,4},{8,11},{9,10},{10,... | collective-permute-start | bytes 69128 | tf_op jit(solution)/shard_map/ppermute | solution.py:130
  11.4 5.0 %collective-permute-start.1 = (f32[32,180]{1,0:T(8,128)S(1)}, f32[32,180]{1,0:T(8,128)S(1)}, u32[]{:S(2)}, u32[]{:S(2)}) collective-permute-start(f32[32,180]{1,0:T(8,128)S(1)} %get-tuple-element.32), channel_id=1, source_target_pairs={{0,2},{1,3},{2,0},{3,1},{4,6},{5,7},{6,4},{7,5},{8,10},{9,11},{10,... | collective-permute-start | bytes 69128 | tf_op jit(solution)/shard_map/ppermute | solution.py:130
  11.4 5.0 %collective-permute-start = (f32[32,180]{1,0:T(8,128)S(1)}, f32[32,180]{1,0:T(8,128)S(1)}, u32[]{:S(2)}, u32[]{:S(2)}) collective-permute-start(f32[32,180]{1,0:T(8,128)S(1)} %get-tuple-element.33), channel_id=1, source_target_pairs={{0,1},{1,0},{2,3},{3,2},{4,5},{5,4},{6,7},{7,6},{8,9},{9,8},{10,11... | collective-permute-start | bytes 69128 | tf_op jit(solution)/shard_map/ppermute | solution.py:130
  12.2 0.7 %copy-start.1 = (s32[256]{0:T(256)S(1)}, s32[256]{0:T(256)}, u32[]{:S(2)}) copy-start(s32[256]{0:T(256)} %param.5) | copy-start | bytes 3076
  27.9 9.6 %all-to-all-start = ((f32[32,4,180]{2,0,1:T(8,128)}), f32[32,4,180]{2,0,1:T(8,128)S(1)}, u32[]{:S(2)}, u32[]{:S(2)}) async-start(f32[32,4,180]{2,0,1:T(8,128)} %copy.37), calls=%async_computation | async-start | bytes 262144 | tf_op jit(solution)/shard_map/all_to_all | solution.py:137
  37.7 9.8 %collective-permute-start.4 = (f32[4,5,32,3]{3,2,1,0:T(8,128)S(1)}, f32[4,5,32,3]{3,2,1,0:T(8,128)S(1)}, u32[]{:S(2)}, u32[]{:S(2)}) collective-permute-start(f32[4,5,32,3]{3,2,1,0:T(8,128)S(1)} %get-tuple-element.13), channel_id=1, source_target_pairs={{1,0},{2,1},{3,2},{0,3},{5,4},{6,5},{7,6},{4,7},{9,8},{10,9},{11,1... | collective-permute-start | bytes 23048 | tf_op jit(solution)/shard_map/ppermute | solution.py:29
  39.4 14.4 %collective-permute-start.3 = (f32[4,5,32,3]{3,2,1,0:T(8,128)S(1)}, f32[4,5,32,3]{3,2,1,0:T(8,128)S(1)}, u32[]{:S(2)}, u32[]{:S(2)}) collective-permute-start(f32[4,5,32,3]{3,2,1,0:T(8,128)S(1)} %get-tuple-element.12), channel_id=1, source_target_pairs={{0,1},{1,2},{2,3},{3,0},{4,5},{5,6},{6,7},{7,4},{8,9},{9,10},{10,1... | collective-permute-start | bytes 23048 | tf_op jit(solution)/shard_map/ppermute | solution.py:27
